TPU v7x, 32 devices: a whole 2x2x4 slice. The times are simulated.
32 devices in a mesh: slab: 2 (over x), blk: 16 (over z, y, core).
Axes of the slice: x: 2, y: 2, z: 4, core: 2. Of those that a mesh axis runs over, the one named last changes fastest.
Arguments:
- transmit: bfloat16 [2, 1024, 2048], P('slab', 'blk'), may hold values from -0.125 to 0.125
- reflect: bfloat16 [2, 2, 1024, 2048], P('slab', None, 'blk'), may hold values from -0.07910156 to 0.07910156
- source_amp: bfloat16 [512, 2048], P('blk'), may hold values from -6 to 6
- source_cell: int32 [512], P('blk'), may hold values from 0 to 1023
- source_slab: int32 [512], P('blk'), may hold values from 0 to 1
Outputs:
- sweep_out: float32 [2, 512, 2048], P('slab', 'blk')
All inputs are finite; a program needn't handle non-finite values.
Results may differ from a plain program's by a relative error of at most 0.018.
Values may be sent and summed in bfloat16 or wider, within the bound.
A program may use at most 64 MiB of HBM per device.

v0:
```python
import jax
import jax.numpy as jnp
from jax import lax
from jax.sharding import PartitionSpec as P


def shifted(block, axis, distance):
    devices = range(lax.axis_size(axis))
    route = [(i - distance, i) for i in devices if i - distance in devices]
    return lax.ppermute(block, axis, route)


def transposed(matrix):
    half_width = matrix.shape[0]
    return jnp.concatenate([matrix[:, :half_width].T, matrix[:, half_width:].T], 1)


def complex_rows(left_rows, right_matrix):
    inner_width = right_matrix.shape[0]
    outer_width = right_matrix.shape[1] // 2
    row_count = left_rows.shape[0]
    stacked = jnp.concatenate([left_rows[:, :inner_width], left_rows[:, inner_width:]], 0)
    product = jnp.dot(stacked, right_matrix, preferred_element_type=jnp.float32)
    real_out = product[:row_count, :outer_width] - product[row_count:, outer_width:]
    imag_out = product[:row_count, outer_width:] + product[row_count:, :outer_width]
    return jnp.concatenate([real_out, imag_out], 1)


def body(transmit, reflect, source_amp, source_cell, source_slab):
    trans_local = transmit[0]
    refl_local = reflect[0]
    half_width = source_amp.shape[1] // 2
    refl_second = lax.all_gather(refl_local[1], "blk", axis=0, tiled=True)
    coupling = complex_rows(refl_local[0], refl_second).astype(jnp.bfloat16)
    start_rows = trans_local.astype(jnp.float32)
    piece_rows = lax.all_gather(trans_local, "blk", axis=0, tiled=True)
    piece_count = piece_rows.shape[0]
    real_cols = lax.slice_in_dim(coupling, 0, piece_count, axis=1)
    imag_cols = lax.dynamic_slice_in_dim(coupling, half_width, piece_count, 1)
    left_rows = jnp.concatenate([real_cols, imag_cols], 1)
    joined = (start_rows + complex_rows(left_rows, piece_rows)).astype(jnp.bfloat16)
    slab_matrix = lax.all_gather(joined, "blk", axis=0, tiled=True)
    back_matrix = transposed(slab_matrix)
    cell_index = lax.iota(jnp.int32, half_width)
    offset = (cell_index[None, :] - source_cell[:, None]) % half_width
    inside = offset < half_width // 4
    here = source_slab == lax.axis_index("slab")
    keep = inside & here[:, None]
    keep = jnp.concatenate([keep, keep], 1)
    forcing = jnp.where(keep, source_amp, jnp.zeros_like(source_amp))
    chain_length = lax.axis_size("slab")
    carried = forcing
    for sweep_step in range(chain_length - 1):
        arrived = shifted(carried, "slab", 1)
        carried = (forcing.astype(jnp.float32) + complex_rows(arrived, slab_matrix)).astype(
            jnp.bfloat16
        )
    current = carried.astype(jnp.float32)
    for sweep_step in range(chain_length - 1):
        message = complex_rows(current.astype(jnp.bfloat16), back_matrix).astype(jnp.bfloat16)
        arrived = shifted(message, "slab", -1)
        current = carried.astype(jnp.float32) + arrived.astype(jnp.float32)
    return current[None]


def solution(mesh):
    return jax.shard_map(
        body,
        mesh=mesh,
        in_specs=(
            P("slab", "blk", None),
            P("slab", None, "blk", None),
            P("blk", None),
            P("blk"),
            P("blk"),
        ),
        out_specs=P("slab", "blk", None),
        check_vma=False,
    )
```

profile of v0, /device:TPU:0, one launch (start us, length us, event | category | flops | bytes accessed | tf_op | source)
XLA Modules:
  0.0 186.9 jit_solution(4141823036874665269)
XLA Ops:
  6.5 0.0 all-gather.8.cloned.1.call-start
  6.5 1.8 slice_bitcast_fusion.2
  8.3 0.0 all-gather.8.cloned.1.call-update
  8.3 0.0 all-gather.10.cloned.1.call-start
  8.4 0.7 all-gather.10.cloned.1.call-update
  9.1 0.0 all-gather.6.cloned.1.call-start
  9.2 53.5 %all-gather.8.cloned.1.call-done = bf16[1,1,1024,2048]{3,2,1,0:T(8,128)(2,1)} async-done(((bf16[1,1,64,2048]{3,2,1,0:T(8,128)(2,1)}), bf16[1,1,1024,2048]{3,2,1,0:T(8,128)(2,1)}) %all-gather.8.cloned.1.call-update) | async-done | bytes 4194320 | tf_op jit(solution)/shard_map/all_gather | solution.py:33
  62.6 2.9 %fusion.6 = f32[128,2048]{1,0:T(8,128)S(1)} fusion(bf16[1,1,1024,2048]{3,2,1,0:T(8,128)(2,1)} %all-gather.8.cloned.1.call-done, bf16[64,1024]{1,0:T(8,128)(2,1)S(1)} %get-tuple-element.18, bf16[64,1024]{1,0:T(8,128)(2,1)S(1)} %get-tuple-element.17), kind=kOutput, calls=%fused_computation.6 | convolution fusion | flops 537395200 | bytes 5505024 | tf_op jit(solution)/shard_map/dot_general | solution.py:23
  65.5 0.0 copy-start.1
  65.5 0.1 fusion.10
  65.6 48.1 %all-gather.10.cloned.1.call-done = bf16[1,1024,2048]{2,1,0:T(8,128)(2,1)} async-done(((bf16[1,64,2048]{2,1,0:T(8,128)(2,1)}), bf16[1,1024,2048]{2,1,0:T(8,128)(2,1)}) %all-gather.10.cloned.1.call-update) | async-done | bytes 4194320 | tf_op jit(solution)/shard_map/all_gather | solution.py:36
  113.7 0.0 copy-start.4
  113.7 0.0 copy-start.3
  113.7 2.9 %fusion.4 = f32[128,2048]{1,0:T(8,128)S(1)} fusion(bf16[1,1024,2048]{2,1,0:T(8,128)(2,1)} %all-gather.10.cloned.1.call-done, bf16[64,1024]{1,0:T(8,128)(2,1)S(1)} %get-tuple-element.10, bf16[64,1024]{1,0:T(8,128)(2,1)S(1)} %get-tuple-element.9), kind=kOutput, calls=%fused_computation.4 | convolution fusion | flops 537395200 | bytes 5505024 | tf_op jit(solution)/shard_map/dot_general | solution.py:23
  116.7 0.1 slice_subtract_fusion
  116.7 0.0 copy-done.1
  116.8 0.8 fusion.8
  117.5 0.0 all-gather.6.cloned.1.call-update
  117.6 0.0 copy-done.4
  117.6 0.0 copy-done.3
  117.6 0.1 fusion.32
  117.7 0.0 copy-done.2
  117.8 3.4 %collective-permute-start = (bf16[32,2048]{1,0:T(8,128)(2,1)S(1)}, bf16[32,2048]{1,0:T(8,128)(2,1)S(1)}, u32[]{:S(2)}, u32[]{:S(2)}) collective-permute-start(bf16[32,2048]{1,0:T(8,128)(2,1)S(1)} %add_select_fusion), channel_id=1, source_target_pairs={{0,16},{1,17},{2,18},{3,19},{4,20},{5,21},{6,22},{7,23},{8,24},{9,... | collective-permute-start | bytes 393224 | tf_op jit(solution)/shard_map/ppermute | solution.py:10
  121.2 3.1 %collective-permute-done = bf16[32,2048]{1,0:T(8,128)(2,1)S(1)} collective-permute-done((bf16[32,2048]{1,0:T(8,128)(2,1)S(1)}, bf16[32,2048]{1,0:T(8,128)(2,1)S(1)}, u32[]{:S(2)}, u32[]{:S(2)}) %collective-permute-start) | collective-permute-done | bytes 131104 | tf_op jit(solution)/shard_map/ppermute | solution.py:10
  124.3 42.3 %all-gather.6.cloned.1.call-done = bf16[1024,2048]{1,0:T(8,128)(2,1)} async-done(((bf16[64,2048]{1,0:T(8,128)(2,1)}), bf16[1024,2048]{1,0:T(8,128)(2,1)}) %all-gather.6.cloned.1.call-update) | async-done | bytes 4194320 | tf_op jit(solution)/shard_map/all_gather | solution.py:42
  166.6 3.2 %fusion.22 = f32[64,2048]{1,0:T(8,128)S(1)} fusion(bf16[1024,2048]{1,0:T(8,128)(2,1)} %all-gather.6.cloned.1.call-done, bf16[32,1024]{1,0:T(8,128)(2,1)S(1)} %get-tuple-element.22, bf16[32,1024]{1,0:T(8,128)(2,1)S(1)} %get-tuple-element.21), kind=kOutput, calls=%fused_computation.40 | convolution fusion | flops 268697600 | bytes 4849664 | tf_op jit(solution)/shard_map/dot_general | solution.py:23
  169.9 0.2 copy-done
  170.1 0.5 slice_bitcast_fusion.1
  170.6 1.4 fusion
  172.1 1.3 collective-permute-start.1
  173.4 6.2 %collective-permute-done.1 = bf16[32,2048]{1,0:T(8,128)(2,1)S(1)} collective-permute-done((bf16[32,2048]{1,0:T(8,128)(2,1)S(1)}, bf16[32,2048]{1,0:T(8,128)(2,1)S(1)}, u32[]{:S(2)}, u32[]{:S(2)}) %collective-permute-start.1) | collective-permute-done | bytes 131104 | tf_op jit(solution)/shard_map/ppermute | solution.py:10
  179.6 0.7 add_bitcast_fusion
  (11 shorter events, 0.2 us)
Async XLA Ops:
  6.5 56.1 %all-gather.8.cloned.1.call-start = ((), (), s32[]{:S(2)}) async-start(), calls=%async_computation.1 | async-start | bytes 4456448 | tf_op jit(solution)/shard_map/all_gather | solution.py:33
  8.3 105.4 %all-gather.10.cloned.1.call-start = ((), (), s32[]{:S(2)}) async-start(), calls=%async_computation.2 | async-start | bytes 4456448 | tf_op jit(solution)/shard_map/all_gather | solution.py:36
  9.1 157.5 %all-gather.6.cloned.1.call-start = ((), (), s32[]{:S(2)}) async-start(), calls=%async_computation | async-start | bytes 4456448 | tf_op jit(solution)/shard_map/all_gather | solution.py:42
  65.5 51.2 %copy-start.1 = (bf16[1,64,2048]{2,1,0:T(8,128)(2,1)S(1)}, bf16[1,64,2048]{2,1,0:T(8,128)(2,1)}, u32[]{:S(2)}) copy-start(bf16[1,64,2048]{2,1,0:T(8,128)(2,1)} %param.5) | copy-start | bytes 786436
  113.7 3.8 %copy-start.4 = (s32[32]{0:T(128)S(1)}, s32[32]{0:T(128)}, u32[]{:S(2)}) copy-start(s32[32]{0:T(128)} %param.9) | copy-start | bytes 388
  113.7 3.9 %copy-start.3 = (s32[32]{0:T(128)S(1)}, s32[32]{0:T(128)}, u32[]{:S(2)}) copy-start(s32[32]{0:T(128)} %param.8) | copy-start | bytes 388
  113.7 4.0 %copy-start.2 = (bf16[32,2048]{1,0:T(8,128)(2,1)S(1)}, bf16[32,2048]{1,0:T(8,128)(2,1)}, u32[]{:S(2)}) copy-start(bf16[32,2048]{1,0:T(8,128)(2,1)} %param.7) | copy-start | bytes 393220
  117.8 6.5 %collective-permute-start = (bf16[32,2048]{1,0:T(8,128)(2,1)S(1)}, bf16[32,2048]{1,0:T(8,128)(2,1)S(1)}, u32[]{:S(2)}, u32[]{:S(2)}) collective-permute-start(bf16[32,2048]{1,0:T(8,128)(2,1)S(1)} %add_select_fusion), channel_id=1, source_target_pairs={{0,16},{1,17},{2,18},{3,19},{4,20},{5,21},{6,22},{7,23},{8,24},{9,... | collective-permute-start | bytes 393224 | tf_op jit(solution)/shard_map/ppermute | solution.py:10
  166.6 3.4 %copy-start = (bf16[1024,2048]{1,0:T(8,128)(2,1)S(1)}, bf16[1024,2048]{1,0:T(8,128)(2,1)}, u32[]{:S(2)}) copy-start(bf16[1024,2048]{1,0:T(8,128)(2,1)} %all-gather.6.cloned.1.call-done) | copy-start | bytes 12582916
  172.1 7.5 %collective-permute-start.1 = (bf16[32,2048]{1,0:T(8,128)(2,1)S(1)}, bf16[32,2048]{1,0:T(8,128)(2,1)S(1)}, u32[]{:S(2)}, u32[]{:S(2)}) collective-permute-start(bf16[32,2048]{1,0:T(8,128)(2,1)S(1)} %pad_maximum_fusion), channel_id=1, source_target_pairs={{16,0},{17,1},{18,2},{19,3},{20,4},{21,5},{22,6},{23,7},{24,8},{25... | collective-permute-start | bytes 393224 | tf_op jit(solution)/shard_map/ppermute | solution.py:10
Sparse Core Ops, SparseCore 0:
  9.5 53.0 all-gather.7
  64.8 48.8 all-gather.9
  117.7 48.8 all-gather.5
where the time goes:
time: 187 us
  waiting for transfers between devices  154 us (82%)
  between operations  13.3 us (7%)
  matrix products  10.4 us (6%)
  starting transfers between devices  4.75 us (3%)
  local copies, waits for them, and re-layouts  2.53 us (1%)
  other arithmetic  1.89 us (1%)
    all_gather x1, waiting for transfers between devices, body(): refl_second = lax.all_gather(refl_local[1], 'blk', axis=0, tiled=True)  53.5 us
    all_gather x1, waiting for transfers between devices, body(): piece_rows = lax.all_gather(trans_local, 'blk', axis=0, tiled=True)  48.1 us
    all_gather x1, waiting for transfers between devices, body(): slab_matrix = lax.all_gather(joined, 'blk', axis=0, tiled=True)  42.3 us
    dot_general x4, matrix products, complex_rows(): product = jnp.dot(stacked, right_matrix, preferred_element_type=jnp.float32)  10.4 us
    ppermute x2, waiting for transfers between devices, shifted(): return lax.ppermute(block, axis, route)  9.38 us
    ppermute x2, starting transfers between devices, shifted(): return lax.ppermute(block, axis, route)  4.67 us
  transfers between devices with their start and end apart: 5, of which 5 were waited for; matrix products, arithmetic and copies ran while one was open for 2% of the time, Pallas kernels for 0%

commit v1 on v0

--- a/solution.py
+++ b/solution.py
@@ -1,6 +1,10 @@
+import functools
+
 import jax
 import jax.numpy as jnp
 from jax import lax
+from jax.experimental import pallas as pl
+from jax.experimental.pallas import tpu as pltpu
 from jax.sharding import PartitionSpec as P
 
 
@@ -63,9 +67,292 @@
     return current[None]
 
 
+MESH = pl.DeviceIdType.MESH
+Y = 2
+CORE = 2
+
+
+def pair_kernel(
+    outer, t_ref, r_ref, amp_ref, cell_ref, slab_ref, out_ref,
+    g_ref, left_ref, coup_ref, x_ref, base_ref, f_ref, d_ref, far_ref,
+    send_sem, recv_sem, far_send, far_recv, own_sem,
+):
+    plane = lax.axis_index("slab")
+    me = lax.axis_index("blk")
+    z, y, core = me // (Y * CORE), (me // CORE) % Y, me % CORE
+    last = 1
+    depth = t_ref.shape[1]
+    width = t_ref.shape[2] // 2
+    half = width // 2
+    sources = amp_ref.shape[0]
+    tile = half // 2
+
+    def blk_of(zz, yy, cc):
+        return (zz * Y + yy) * CORE + cc
+
+    z_peers = [(z + step) % outer for step in range(1, outer)]
+    y_peer, c_peer, x_peer = 1 - y, 1 - core, 1 - plane
+
+    def rows(block):
+        return pl.ds(pl.multiple_of(block * depth, depth), depth)
+
+    def at(dev, pl_id=None):
+        return (plane if pl_id is None else pl_id, dev)
+
+    def pieces(h):
+        lo = h * half
+        out = []
+        for m, src in ((0, r_ref.at[0, 1]), (1, t_ref.at[0])):
+            for part in range(2):
+                out.append((src.at[:, part * width + lo:part * width + lo + half],
+                            g_ref.at[m, part, rows(me)]))
+        for part in range(2):
+            out.append((r_ref.at[0, 0, :, part * width:(part + 1) * width],
+                        left_ref.at[part * depth:(part + 1) * depth]))
+        return out
+
+    def local_piece(i):
+        src, dst = pieces(1)[i]
+        return pltpu.make_async_copy(src, dst, own_sem.at[i])
+
+    def cross_piece(i):
+        src, dst = pieces(0)[i]
+        return pltpu.make_async_remote_copy(
+            src_ref=src, dst_ref=dst, send_sem=far_send.at[i], recv_sem=far_recv.at[i],
+            device_id=at(me, 0), device_id_type=MESH)
+
+    @pl.when(plane == last)
+    def _():
+        for i in range(6):
+            local_piece(i).start()
+
+    barrier = pltpu.get_barrier_semaphore()
+    peers = [at(blk_of(p, y, core)) for p in z_peers]
+    peers += [at(blk_of(z, y_peer, core)), at(blk_of(z, y, c_peer)), at(me, x_peer)]
+    for peer in peers:
+        pl.semaphore_signal(barrier, inc=1, device_id=peer, device_id_type=MESH)
+    pl.semaphore_wait(barrier, len(peers))
+
+    @pl.when(plane == last)
+    def _():
+        for i in range(6):
+            cross_piece(i).start()
+
+    def own_ready(first, count):
+        @pl.when(plane == last)
+        def _():
+            for i in range(first, first + count):
+                local_piece(i).wait()
+
+        @pl.when(plane != last)
+        def _():
+            for i in range(first, first + count):
+                cross_piece(i).wait_recv()
+
+    pending = []
+    used = [0, 0, 0]
+
+    def push(m, block, dev):
+        k = used[m]
+        used[m] += 1
+        ref = g_ref.at[m, :, rows(block)]
+        copy = pltpu.make_async_remote_copy(
+            src_ref=ref, dst_ref=ref, send_sem=send_sem.at[m, k],
+            recv_sem=recv_sem.at[m, block], device_id=at(dev), device_id_type=MESH)
+        copy.start()
+        pending.append(copy)
+
+    def landed(m, block):
+        ref = g_ref.at[m, :, rows(block)]
+        pltpu.make_async_remote_copy(
+            src_ref=ref, dst_ref=ref, send_sem=send_sem.at[m, 0],
+            recv_sem=recv_sem.at[m, block], device_id=at(blk_of(z, y, c_peer)),
+            device_id_type=MESH).wait_recv()
+
+    y_dev, c_dev = blk_of(z, y_peer, core), blk_of(z, y, c_peer)
+
+    def spread_own(m):
+        for p in z_peers:
+            push(m, me, blk_of(p, y, core))
+        push(m, me, y_dev)
+        push(m, me, c_dev)
+
+    def spread_z(m):
+        for p in reversed(z_peers):
+            block = blk_of(p, y, core)
+            landed(m, block)
+            push(m, block, y_dev)
+            push(m, block, c_dev)
+
+    def spread_y(m):
+        for p in [z] + z_peers[::-1]:
+            block = blk_of(p, y_peer, core)
+            landed(m, block)
+            push(m, block, c_dev)
+
+    def finish(m):
+        for p in [z] + z_peers:
+            for yy in (y, y_peer):
+                landed(m, blk_of(p, yy, c_peer))
+
+    def complex_tile(lhs, m, j):
+        cols = pl.ds(pl.multiple_of(j * tile, tile), tile)
+        n = lhs.shape[0] // 2
+        pr = jnp.dot(lhs, g_ref[m, 0, :, cols], preferred_element_type=jnp.float32)
+        pi = jnp.dot(lhs, g_ref[m, 1, :, cols], preferred_element_type=jnp.float32)
+        return pr[:n] - pi[n:], pi[:n] + pr[n:]
+
+    mine = pl.multiple_of(plane * half, half)
+    other = pl.multiple_of(x_peer * half, half)
+
+    own_ready(0, 2)
+    spread_own(0)
+    own_ready(2, 2)
+    spread_own(1)
+
+    eye = (lax.broadcasted_iota(jnp.int32, (sources, sources), 0)
+           == lax.broadcasted_iota(jnp.int32, (sources, sources), 1))
+    cell = jnp.sum(jnp.where(eye, cell_ref[...], 0), axis=1, keepdims=True)
+    slab = jnp.sum(jnp.where(eye, slab_ref[...], 0), axis=1, keepdims=True)
+    col = lax.broadcasted_iota(jnp.int32, (sources, width), 1)
+    offset = col - cell
+    offset = jnp.where(offset < 0, offset + width, offset)
+    inside = offset < width // 4
+    for part in range(2):
+        amp = amp_ref[:, part * width:(part + 1) * width].astype(jnp.float32)
+        spot = slice(part * sources, (part + 1) * sources)
+        x_ref[spot, :] = jnp.where(inside & (slab == 0), amp, 0.0).astype(jnp.bfloat16)
+        base_ref[spot, :] = jnp.where(inside & (slab == 1), amp, 0.0)
+
+    spread_z(0)
+    spread_y(0)
+    spread_z(1)
+    finish(0)
+    own_ready(4, 2)
+
+    @pl.loop(0, half // tile)
+    def _(j):
+        re, im = complex_tile(left_ref[...], 0, j)
+        cols = pl.ds(pl.multiple_of(mine + j * tile, tile), tile)
+        coup_ref[0:depth, cols] = re.astype(jnp.bfloat16)
+        coup_ref[depth:2 * depth, cols] = im.astype(jnp.bfloat16)
+
+    def swap(ref, i):
+        return pltpu.make_async_remote_copy(
+            src_ref=ref, dst_ref=ref, send_sem=far_send.at[i], recv_sem=far_recv.at[i],
+            device_id=at(me, x_peer), device_id_type=MESH)
+
+    coup_copy = swap(coup_ref.at[:, pl.ds(mine, half)], 6)
+    coup_copy.start()
+    spread_y(1)
+    finish(1)
+    swap(coup_ref.at[:, pl.ds(other, half)], 6).wait_recv()
+
+    @pl.loop(0, half // tile)
+    def _(j):
+        re, im = complex_tile(coup_ref[...], 1, j)
+        cols = pl.ds(pl.multiple_of(j * tile, tile), tile)
+        here = rows(me)
+        g_ref[2, 0, here, cols] = (re + g_ref[1, 0, here, cols].astype(jnp.float32)).astype(jnp.bfloat16)
+        g_ref[2, 1, here, cols] = (im + g_ref[1, 1, here, cols].astype(jnp.float32)).astype(jnp.bfloat16)
+
+    spread_own(2)
+    spread_z(2)
+    spread_y(2)
+    finish(2)
+
+    @pl.loop(0, half // tile)
+    def _(j):
+        re, im = complex_tile(x_ref[...], 2, j)
+        cols = pl.ds(pl.multiple_of(mine + j * tile, tile), tile)
+        f_ref[0:sources, cols] = (re + base_ref[0:sources, cols]).astype(jnp.bfloat16)
+        f_ref[sources:, cols] = (im + base_ref[sources:, cols]).astype(jnp.bfloat16)
+
+    @pl.when(plane != last)
+    def _():
+        swap(f_ref.at[:, pl.ds(mine, half)], 7).start()
+
+    step_rows = width // 4
+
+    @pl.loop(0, 4)
+    def _(j):
+        spots = pl.ds(pl.multiple_of(j * step_rows, step_rows), step_rows)
+        lhs = f_ref[:, pl.ds(mine, half)]
+        dims = (((1,), (1,)), ((), ()))
+        pr = lax.dot_general(lhs, g_ref[2, 0, spots, :], dims, preferred_element_type=jnp.float32)
+        pi = lax.dot_general(lhs, g_ref[2, 1, spots, :], dims, preferred_element_type=jnp.float32)
+        d_ref[0:sources, spots] = (pr[:sources] - pi[sources:]).astype(d_ref.dtype)
+        d_ref[sources:, spots] = (pi[:sources] + pr[sources:]).astype(d_ref.dtype)
+
+    def message(pl_id):
+        return pltpu.make_async_remote_copy(
+            src_ref=d_ref, dst_ref=far_ref, send_sem=far_send.at[8], recv_sem=far_recv.at[8],
+            device_id=at(me, pl_id), device_id_type=MESH)
+
+    @pl.when(plane == last)
+    def _():
+        message(0).start()
+        swap(f_ref.at[:, pl.ds(other, half)], 7).wait_recv()
+        out_ref[:, :width] = f_ref[:sources].astype(jnp.float32)
+        out_ref[:, width:] = f_ref[sources:].astype(jnp.float32)
+        message(0).wait_send()
+        for i in range(6):
+            cross_piece(i).wait_send()
+
+    @pl.when(plane != last)
+    def _():
+        message(0).wait_recv()
+        for part in range(2):
+            spot = slice(part * sources, (part + 1) * sources)
+            total = d_ref[spot].astype(jnp.float32) + far_ref[spot].astype(jnp.float32)
+            out_ref[:, part * width:(part + 1) * width] = (
+                x_ref[spot].astype(jnp.float32) + total.astype(jnp.bfloat16).astype(jnp.float32))
+        swap(f_ref.at[:, pl.ds(mine, half)], 7).wait_send()
+
+    coup_copy.wait_send()
+    for copy in pending:
+        copy.wait_send()
+
+
+def pair_body(transmit, reflect, source_amp, source_cell, source_slab):
+    outer = lax.axis_size("blk") // (Y * CORE)
+    sources, double = source_amp.shape
+    depth = transmit.shape[1]
+    width = double // 2
+    sends = 4 * outer - 1
+    vm = pl.BlockSpec(memory_space=pltpu.VMEM)
+    hbm = pl.BlockSpec(memory_space=pl.ANY)
+    bf16 = jnp.bfloat16
+    out = pl.pallas_call(
+        functools.partial(pair_kernel, outer),
+        out_shape=jax.ShapeDtypeStruct((sources, double), jnp.float32),
+        in_specs=[hbm, hbm, vm, vm, vm],
+        out_specs=vm,
+        scratch_shapes=[
+            pltpu.VMEM((3, 2, width, width // 2), bf16),
+            pltpu.VMEM((2 * depth, width), bf16),
+            pltpu.VMEM((2 * depth, width), bf16),
+            pltpu.VMEM((2 * sources, width), bf16),
+            pltpu.VMEM((2 * sources, width), jnp.float32),
+            pltpu.VMEM((2 * sources, width), bf16),
+            pltpu.VMEM((2 * sources, width), bf16),
+            pltpu.VMEM((2 * sources, width), bf16),
+            pltpu.SemaphoreType.DMA((3, sends)),
+            pltpu.SemaphoreType.DMA((3, lax.axis_size("blk"))),
+            pltpu.SemaphoreType.DMA((9,)),
+            pltpu.SemaphoreType.DMA((9,)),
+            pltpu.SemaphoreType.DMA((6,)),
+        ],
+        compiler_params=pltpu.CompilerParams(
+            collective_id=0, has_side_effects=True, vmem_limit_bytes=40 * 2**20),
+    )(transmit, reflect, source_amp, source_cell[None], source_slab[None])
+    return out[None]
+
+
 def solution(mesh):
+    pair = mesh.shape["slab"] == 2 and mesh.shape["blk"] % (Y * CORE) == 0
     return jax.shard_map(
-        body,
+        pair_body if pair else body,
         mesh=mesh,
         in_specs=(
             P("slab", "blk", None),

time: 187 us -> 73.6 us (0.39)
  waiting for transfers between devices: 154 us -> 0 us
  Pallas kernels: 0 us -> 69.1 us
  between operations: 13.3 us -> 0.01 us
  matrix products: 10.4 us -> 0 us
  starting transfers between devices: 4.75 us -> 0 us
  other arithmetic: 1.89 us -> 0 us
    all_gather x3 -> x0, waiting for transfers between devices: 144 us -> none  [the longest x1 53.5 us: body(): refl_second = lax.all_gather(refl_local[1], 'blk', axis=0, tiled=True)]
    pallas_call x0 -> x1, Pallas kernels: none -> 69.1 us  [pair_body(): pl.pallas_call(functools.partial(pair_kernel, outer), out_shape=jax.Shape...]
    dot_general x4 -> x0, matrix products: 10.4 us -> none  [complex_rows(): product = jnp.dot(stacked, right_matrix, preferred_element_type=jnp.float32)]
    ppermute x2 -> x0, waiting for transfers between devices: 9.38 us -> none  [shifted(): return lax.ppermute(block, axis, route)]
    ppermute x2 -> x0, starting transfers between devices: 4.67 us -> none  [shifted(): return lax.ppermute(block, axis, route)]
    unnamed x10 -> x11, local copies, waits for them, and re-layouts: 0.19 us -> 4.27 us
  transfers between devices with their start and end apart: 5 -> 0, of which waited for: 5 -> 0; matrix products, arithmetic and copies ran while one was open for 2% -> 0% of each run, Pallas kernels for 0% -> 0%
where the time goes in v1:
time: 73.6 us; the launch traced here: 73.4 us
  Pallas kernels  69.1 us (94%)
  local copies, waits for them, and re-layouts  4.27 us (6%)
    pallas_call x1, Pallas kernels, pair_body(): pl.pallas_call(functools.partial(pair_kernel, outer), out_shape=jax.Shape...  69.1 us
    unnamed x11, local copies, waits for them, and re-layouts  4.27 us

profile of v1, /device:TPU:0, one launch (start us, length us, event | category | flops | bytes accessed | tf_op | source)
XLA Modules:
  0.0 73.4 jit_solution(16324295705435555320)
XLA Ops:
  0.0 0.0 copy-start.3
  0.0 0.0 copy-start.4
  0.0 0.7 copy-done.3
  0.7 0.0 copy-done.4
  0.7 0.0 copy-start
  0.7 1.0 %copy-done = bf16[1,2,64,2048]{3,2,1,0:T(8,128)(2,1)S(1)} copy-done((bf16[1,2,64,2048]{3,2,1,0:T(8,128)(2,1)S(1)}, bf16[1,2,64,2048]{3,2,1,0:T(8,128)(2,1)}, u32[]{:S(2)}) %copy-start) | copy-done | bytes 524312
  1.7 0.0 copy-start.1
  1.7 0.9 %copy-done.1 = bf16[1,64,2048]{2,1,0:T(8,128)(2,1)S(1)} copy-done((bf16[1,64,2048]{2,1,0:T(8,128)(2,1)S(1)}, bf16[1,64,2048]{2,1,0:T(8,128)(2,1)}, u32[]{:S(2)}) %copy-start.1) | copy-done | bytes 262168
  2.7 0.0 copy-start.2
  2.7 0.9 %copy-done.2 = bf16[32,2048]{1,0:T(8,128)(2,1)S(1)} copy-done((bf16[32,2048]{1,0:T(8,128)(2,1)S(1)}, bf16[32,2048]{1,0:T(8,128)(2,1)}, u32[]{:S(2)}) %copy-start.2) | copy-done | bytes 131096
  3.6 69.1 %shard_map.55 = f32[32,2048]{1,0:T(8,128)S(1)} custom-call(bf16[1,64,2048]{2,1,0:T(8,128)(2,1)S(1)} %copy-done.1, bf16[1,2,64,2048]{3,2,1,0:T(8,128)(2,1)S(1)} %copy-done, bf16[32,2048]{1,0:T(8,128)(2,1)S(1)} %copy-done.2, s32[1,32]{1,0:T(1,128)S(1)} %bitcast.4, s32[1,32]{1,0:T(1,128)S(1)} %bitcast.5), custom_call_target="tpu_custom_call" | custom-call | tf_op jit(solution)/shard_map/pallas_call | solution.py:326
  72.7 0.7 copy.7
Async XLA Ops:
  0.0 0.7 copy-start.3
  0.0 0.7 copy-start.4
  0.7 1.0 %copy-start = (bf16[1,2,64,2048]{3,2,1,0:T(8,128)(2,1)S(1)}, bf16[1,2,64,2048]{3,2,1,0:T(8,128)(2,1)}, u32[]{:S(2)}) copy-start(bf16[1,2,64,2048]{3,2,1,0:T(8,128)(2,1)} %r_ref.1) | copy-start | bytes 1572868
  1.7 0.9 %copy-start.1 = (bf16[1,64,2048]{2,1,0:T(8,128)(2,1)S(1)}, bf16[1,64,2048]{2,1,0:T(8,128)(2,1)}, u32[]{:S(2)}) copy-start(bf16[1,64,2048]{2,1,0:T(8,128)(2,1)} %t_ref.1) | copy-start | bytes 786436
  2.7 0.9 %copy-start.2 = (bf16[32,2048]{1,0:T(8,128)(2,1)S(1)}, bf16[32,2048]{1,0:T(8,128)(2,1)}, u32[]{:S(2)}) copy-start(bf16[32,2048]{1,0:T(8,128)(2,1)} %amp_ref.1) | copy-start | bytes 393220

commit v2 on v0

--- a/solution.py
+++ b/solution.py
@@ -1,6 +1,10 @@
+import functools
+
 import jax
 import jax.numpy as jnp
 from jax import lax
+from jax.experimental import pallas as pl
+from jax.experimental.pallas import tpu as pltpu
 from jax.sharding import PartitionSpec as P
 
 
@@ -63,9 +67,408 @@
     return current[None]
 
 
+MESH = pl.DeviceIdType.MESH
+Y = 2
+CORE = 2
+PLANES = 2
+
+
+def pair_kernel(
+    outer, t_hbm, r_hbm, amp_hbm, cell_hbm, slab_hbm, out_ref,
+    amp_ref, cell_ref, slab_ref, g_ref, left_ref, coup_ref, x_ref, base_ref,
+    f_ref, whole_ref, d_ref, far_ref,
+    arg_sem, in_send, in_recv, left_send, left_recv, z_send, z_recv,
+    c_send, c_recv, x_send, x_recv, f_send, f_recv, d_send, d_recv,
+):
+    plane = lax.axis_index("slab")
+    me = lax.axis_index("blk")
+    z, y, core = me // (Y * CORE), (me // CORE) % Y, me % CORE
+    last = PLANES - 1
+    depth = t_hbm.shape[1]
+    width = t_hbm.shape[2] // 2
+    part_width = width // (PLANES * Y)
+    sources = amp_hbm.shape[0]
+    y_peer, c_peer, x_peer = 1 - y, 1 - core, 1 - plane
+    q = plane * Y + y
+    f32, bf16 = jnp.float32, jnp.bfloat16
+
+    def dev(p, zz, yy, cc):
+        return (p, (zz * Y + yy) * CORE + cc)
+
+    def cols(quarter, base=0):
+        return pl.ds(pl.multiple_of(base + quarter * part_width, part_width), part_width)
+
+    def remote(s, d, ss, rs, to):
+        return pltpu.make_async_remote_copy(
+            src_ref=s, dst_ref=d, send_sem=ss, recv_sem=rs, device_id=to, device_id_type=MESH)
+
+    def piece(m, part, p, yy):
+        s = r_hbm.at[0, 1] if m == 0 else t_hbm.at[0]
+        return s.at[:, cols(p * Y + yy, part * width)]
+
+    def slot(m, part, yy):
+        return g_ref.at[m, part].at[z * Y + yy, core]
+
+    def piece_local(m, part):
+        return pltpu.make_async_copy(piece(m, part, last, y), slot(m, part, y), in_recv.at[(m * 2 + part) * Y + y])
+
+    targets = ((0, y), (0, y_peer), (last, y_peer))
+
+    def piece_send(m, part, k):
+        p, yy = targets[k]
+        return remote(piece(m, part, p, yy), slot(m, part, y), in_send.at[m, part, k],
+                      in_recv.at[(m * 2 + part) * Y + y], dev(p, z, yy, core))
+
+    def piece_recv(m, part, yy):
+        return remote(slot(m, part, yy), slot(m, part, yy), in_send.at[m, part, 0],
+                      in_recv.at[(m * 2 + part) * Y + yy], dev(plane, z, y_peer, core))
+
+    def left_src(part):
+        return r_hbm.at[0, 0, :, part * width:(part + 1) * width]
+
+    def left_local(part):
+        return pltpu.make_async_copy(left_src(part), left_ref.at[part].at[y], left_recv.at[part * Y + y])
+
+    def left_push(part, k):
+        to = dev(0, z, y, core) if k == 0 else dev(last, z, y_peer, core)
+        return remote(left_src(part), left_ref.at[part].at[y], left_send.at[part, k],
+                      left_recv.at[part * Y + y], to)
+
+    def left_relay(part, yy):
+        ref = left_ref.at[part].at[yy]
+        return remote(ref, ref, left_send.at[part, 0], left_recv.at[part * Y + yy],
+                      dev(plane, z, y_peer, core))
+
+    args = [pltpu.make_async_copy(a, b, arg_sem.at[i]) for i, (a, b) in enumerate(
+        ((amp_hbm, amp_ref), (cell_hbm, cell_ref), (slab_hbm, slab_ref)))]
+    for copy in args:
+        copy.start()
+
+    @pl.when(plane == last)
+    def _():
+        for m in range(2):
+            for part in range(2):
+                piece_local(m, part).start()
+        for part in range(2):
+            left_local(part).start()
+
+    barrier = pltpu.get_barrier_semaphore()
+    peers = [dev(plane, (z + step) % outer, y, core) for step in range(1, outer)]
+    peers += [dev(plane, z, y, c_peer), dev(plane, z, y_peer, core),
+              dev(x_peer, z, y, core), dev(x_peer, z, y_peer, core)]
+    for peer in peers:
+        pl.semaphore_signal(barrier, inc=1, device_id=peer, device_id_type=MESH)
+    pl.semaphore_wait(barrier, len(peers))
+
+    @pl.when(plane == last)
+    def _():
+        for part in range(2):
+            for k in range(3):
+                piece_send(0, part, k).start()
+        for part in range(2):
+            for k in range(2):
+                left_push(part, k).start()
+        for part in range(2):
+            for k in range(3):
+                piece_send(1, part, k).start()
+
+    def pieces_ready(m):
+        for part in range(2):
+            @pl.when(plane == last)
+            def _():
+                piece_local(m, part).wait()
+
+            @pl.when(plane != last)
+            def _():
+                piece_recv(m, part, y).wait_recv()
+
+            piece_recv(m, part, y_peer).wait_recv()
+
+    pending = []
+    always = plane >= 0
+    steps = [s for d in range(1, outer) for s in (d, -d)]
+    near = [s for s in steps if abs(s) <= 2]
+
+    def chunk(m, zz, cc):
+        return g_ref.at[m].at[:, pl.ds(zz * Y, Y), cc]
+
+    def push(m, k, shift, to, ok):
+        zz = z + shift
+        ref = chunk(m, zz, core)
+        copy = remote(ref, ref, z_send.at[m, k], z_recv.at[(m * outer + zz) * CORE + core], to)
+        copy.start()
+        pending.append((ok, m, k, shift))
+
+    def landed(m, zz, cc):
+        ref = chunk(m, zz, cc)
+        remote(ref, ref, z_send.at[m, 0], z_recv.at[(m * outer + zz) * CORE + cc],
+               dev(plane, z, y, c_peer)).wait_recv()
+
+    def valid(zz):
+        return (zz >= 0) & (zz < outer)
+
+    def spread_own(m):
+        for k, s in enumerate(sorted(near, key=lambda v: -abs(v))):
+            ok = valid(z + s)
+
+            @pl.when(ok)
+            def _():
+                push(m, k, 0, dev(plane, z + s, y, core), ok)
+        push(m, 4, 0, dev(plane, z, y, c_peer), always)
+
+    def spread(m, chosen):
+        for s in chosen:
+            i = steps.index(s)
+            ok = valid(z + s)
+
+            @pl.when(ok)
+            def _():
+                landed(m, z + s, core)
+            if abs(s) >= 2:
+                onward = 1 if s < 0 else -1
+                both = ok & valid(z + onward)
+
+                @pl.when(both)
+                def _():
+                    push(m, 5 + len(steps) + i, s, dev(plane, z + onward, y, core), both)
+
+            @pl.when(ok)
+            def _():
+                push(m, 5 + i, s, dev(plane, z, y, c_peer), ok)
+
+    def finish(m):
+        for zz in range(outer):
+            landed(m, zz, c_peer)
+
+    def side(m, part):
+        return g_ref[m, part].reshape(width, part_width)
+
+    def complex_rows_here(lhs, m):
+        n = lhs.shape[0] // 2
+        pr = jnp.dot(lhs, side(m, 0), preferred_element_type=f32)
+        pi = jnp.dot(lhs, side(m, 1), preferred_element_type=f32)
+        return pr[:n] - pi[n:], pi[:n] + pr[n:]
+
+    seconds = [s for s in steps if abs(s) == 2]
+    firsts = [s for s in steps if abs(s) == 1]
+    rest = [s for s in steps if abs(s) > 2]
+
+    for copy in args:
+        copy.wait()
+    eye = (lax.broadcasted_iota(jnp.int32, (sources, sources), 0)
+           == lax.broadcasted_iota(jnp.int32, (sources, sources), 1))
+    cell = jnp.sum(jnp.where(eye, cell_ref[...], 0), axis=1, keepdims=True)
+    slab = jnp.sum(jnp.where(eye, slab_ref[...], 0), axis=1, keepdims=True)
+    offset = lax.broadcasted_iota(jnp.int32, (sources, width), 1) - cell
+    offset = jnp.where(offset < 0, offset + width, offset)
+    inside = offset < width // 4
+    for part in range(2):
+        amp = amp_ref[:, part * width:(part + 1) * width].astype(f32)
+        x_ref[part, y] = jnp.where(inside & (slab == 0), amp, 0.0).astype(bf16)
+        base_ref[part, y] = jnp.where(inside & (slab == 1), amp, 0.0).astype(bf16)
+
+    pieces_ready(0)
+    spread_own(0)
+
+    def x_swap(yy):
+        ref = x_ref.at[:, yy]
+        return remote(ref, ref, x_send.at[0], x_recv.at[0], dev(plane, z, y_peer, core))
+
+    def base_swap(yy, quarter):
+        ref = base_ref.at[:, yy, :, cols(quarter)]
+        return remote(ref, ref, x_send.at[1], x_recv.at[1], dev(plane, z, y_peer, core))
+
+    x_swap(y).start()
+    base_swap(y, plane * Y + y_peer).start()
+
+    for part in range(2):
+        @pl.when(plane == last)
+        def _():
+            left_local(part).wait()
+
+        @pl.when(plane != last)
+        def _():
+            left_relay(part, y).wait_recv()
+            left_relay(part, y).start()
+
+    spread(0, seconds)
+    pieces_ready(1)
+    spread_own(1)
+    spread(0, firsts + rest)
+    finish(0)
+    for part in range(2):
+        left_relay(part, y_peer).wait_recv()
+
+    re, im = complex_rows_here(left_ref[...].reshape(2 * Y * depth, width), 0)
+    coup_ref[0:Y * depth, cols(q)] = re.astype(bf16)
+    coup_ref[Y * depth:, cols(q)] = im.astype(bf16)
+    others = ((x_peer, y), (plane, y_peer), (x_peer, y_peer))
+
+    def coup_copy(k, quarter):
+        p, yy = others[k]
+        ref = coup_ref.at[:, cols(quarter)]
+        return remote(ref, ref, c_send.at[k], c_recv.at[quarter], dev(p, z, yy, core))
+
+    for k in range(3):
+        coup_copy(k, q).start()
+    spread(1, seconds + firsts + rest)
+    finish(1)
+    for k, (p, yy) in enumerate(others):
+        coup_copy(k, p * Y + yy).wait_recv()
+
+    re, im = complex_rows_here(coup_ref[...], 1)
+    for part, value in ((0, re), (1, im)):
+        start = g_ref[1, part, pl.ds(z * Y, Y), core].reshape(Y * depth, part_width)
+        joined = (value + start.astype(f32)).astype(bf16)
+        g_ref[2, part, pl.ds(z * Y, Y), core] = joined.reshape(Y, depth, part_width)
+    spread_own(2)
+    spread(2, seconds + firsts + rest)
+    x_swap(y_peer).wait_recv()
+    base_swap(y_peer, q).wait_recv()
+    finish(2)
+
+    re, im = complex_rows_here(x_ref[...].reshape(2 * Y * sources, width), 2)
+    for part, value in ((0, re), (1, im)):
+        start = base_ref[part, :, :, cols(q)].astype(f32)
+        f_ref[part] = (value.reshape(Y, sources, part_width) + start).astype(bf16)
+
+    lhs = f_ref[...].reshape(2 * Y * sources, part_width)
+    n = Y * sources
+    tile = Y * CORE * depth
+
+    @pl.loop(0, outer)
+    def _(j):
+        spots = pl.ds(pl.multiple_of(j * tile, tile), tile)
+        dims = (((1,), (1,)), ((), ()))
+        right = [g_ref[2, part, pl.ds(j * Y, Y)].reshape(tile, part_width) for part in range(2)]
+        pr = lax.dot_general(lhs, right[0], dims, preferred_element_type=f32)
+        pi = lax.dot_general(lhs, right[1], dims, preferred_element_type=f32)
+        d_ref[0, :, :, spots] = (pr[:n] - pi[n:]).astype(bf16).reshape(Y, sources, tile)
+        d_ref[1, :, :, spots] = (pi[:n] + pr[n:]).astype(bf16).reshape(Y, sources, tile)
+
+    def d_copy(k, yy, quarter):
+        return remote(d_ref.at[:, yy], far_ref.at[quarter], d_send.at[k], d_recv.at[quarter],
+                      dev(0, z, yy, core))
+
+    def f_copy(k, yy, quarter):
+        return remote(f_ref.at[:, yy], whole_ref.at[:, :, cols(quarter)], f_send.at[k],
+                      f_recv.at[quarter], dev(last, z, yy, core))
+
+    d_copy(0, y_peer, q).start()
+
+    @pl.when(plane == last)
+    def _():
+        d_copy(1, y, q).start()
+
+    f_copy(0, y_peer, q).start()
+
+    @pl.when(plane != last)
+    def _():
+        f_copy(1, y, q).start()
+
+    @pl.when(plane == last)
+    def _():
+        whole_ref[:, :, cols(q)] = f_ref[:, y]
+        for p, yy in others:
+            f_copy(0, y, p * Y + yy).wait_recv()
+        for part in range(2):
+            out_ref[:, part * width:(part + 1) * width] = whole_ref[part].astype(f32)
+
+    @pl.when(plane != last)
+    def _():
+        for p, yy in others:
+            d_copy(0, y, p * Y + yy).wait_recv()
+        for part in range(2):
+            total = d_ref.at[part][y].astype(f32)
+            for p, yy in others:
+                total = total + far_ref.at[p * Y + yy][part].astype(f32)
+            out_ref[:, part * width:(part + 1) * width] = (
+                x_ref.at[part][y].astype(f32) + total.astype(bf16).astype(f32))
+
+    @pl.when(plane == last)
+    def _():
+        d_copy(1, y, q).wait_send()
+        for m in range(2):
+            for part in range(2):
+                for k in range(3):
+                    piece_send(m, part, k).wait_send()
+        for part in range(2):
+            for k in range(2):
+                left_push(part, k).wait_send()
+
+    @pl.when(plane != last)
+    def _():
+        f_copy(1, y, q).wait_send()
+        for part in range(2):
+            left_relay(part, y).wait_send()
+
+    d_copy(0, y_peer, q).wait_send()
+    f_copy(0, y_peer, q).wait_send()
+    x_swap(y).wait_send()
+    base_swap(y, plane * Y + y_peer).wait_send()
+    for k in range(3):
+        coup_copy(k, q).wait_send()
+    for ok, m, k, shift in pending:
+        @pl.when(ok)
+        def _():
+            ref = chunk(m, z + shift, core)
+            remote(ref, ref, z_send.at[m, k], z_recv.at[(m * outer + z + shift) * CORE + core],
+                   dev(plane, z, y, c_peer)).wait_send()
+
+
+def pair_body(transmit, reflect, source_amp, source_cell, source_slab):
+    outer = lax.axis_size("blk") // (Y * CORE)
+    sources, double = source_amp.shape
+    depth = transmit.shape[1]
+    width = double // 2
+    quarter = width // (PLANES * Y)
+    bf16 = jnp.bfloat16
+    hbm = pl.BlockSpec(memory_space=pltpu.HBM)
+    sem = pltpu.SemaphoreType.DMA
+    out = pl.pallas_call(
+        functools.partial(pair_kernel, outer),
+        out_shape=jax.ShapeDtypeStruct((sources, double), jnp.float32),
+        in_specs=[hbm] * 5,
+        out_specs=pl.BlockSpec(memory_space=pltpu.VMEM),
+        scratch_shapes=[
+            pltpu.VMEM((sources, double), bf16),
+            pltpu.VMEM((1, sources), jnp.int32),
+            pltpu.VMEM((1, sources), jnp.int32),
+            pltpu.VMEM((3, 2, outer * Y, CORE, depth, quarter), bf16),
+            pltpu.VMEM((2, Y, depth, width), bf16),
+            pltpu.VMEM((2 * Y * depth, width), bf16),
+            pltpu.VMEM((2, Y, sources, width), bf16),
+            pltpu.VMEM((2, Y, sources, width), bf16),
+            pltpu.VMEM((2, Y, sources, quarter), bf16),
+            pltpu.VMEM((2, sources, width), bf16),
+            pltpu.VMEM((2, Y, sources, width), bf16),
+            pltpu.VMEM((PLANES * Y, 2, sources, width), bf16),
+            sem((3,)),
+            sem((2, 2, 3)),
+            sem((2 * 2 * Y,)),
+            sem((2, 2)),
+            sem((2 * Y,)),
+            sem((3, 5 + 4 * (outer - 1))),
+            sem((3 * outer * CORE,)),
+            sem((3,)),
+            sem((PLANES * Y,)),
+            sem((2,)),
+            sem((2,)),
+            sem((2,)),
+            sem((PLANES * Y,)),
+            sem((2,)),
+            sem((PLANES * Y,)),
+        ],
+        compiler_params=pltpu.CompilerParams(
+            collective_id=0, has_side_effects=True, vmem_limit_bytes=67043328),
+    )(transmit, reflect, source_amp, source_cell[None], source_slab[None])
+    return out[None]
+
+
 def solution(mesh):
+    pair = mesh.shape["slab"] == PLANES and mesh.shape["blk"] % (Y * CORE) == 0
     return jax.shard_map(
-        body,
+        pair_body if pair else body,
         mesh=mesh,
         in_specs=(
             P("slab", "blk", None),

time: 187 us -> 55.5 us (0.30)
  waiting for transfers between devices: 154 us -> 0 us
  Pallas kernels: 0 us -> 53.7 us
  between operations: 13.3 us -> 0.01 us
  matrix products: 10.4 us -> 0 us
  starting transfers between devices: 4.75 us -> 0 us
  other arithmetic: 1.89 us -> 0 us
    all_gather x3 -> x0, waiting for transfers between devices: 144 us -> none  [the longest x1 53.5 us: body(): refl_second = lax.all_gather(refl_local[1], 'blk', axis=0, tiled=True)]
    pallas_call x0 -> x1, Pallas kernels: none -> 53.7 us  [pair_body(): pl.pallas_call(functools.partial(pair_kernel, outer), out_shape=jax.Shape...]
    dot_general x4 -> x0, matrix products: 10.4 us -> none  [complex_rows(): product = jnp.dot(stacked, right_matrix, preferred_element_type=jnp.float32)]
    ppermute x2 -> x0, waiting for transfers between devices: 9.38 us -> none  [shifted(): return lax.ppermute(block, axis, route)]
    ppermute x2 -> x0, starting transfers between devices: 4.67 us -> none  [shifted(): return lax.ppermute(block, axis, route)]
  transfers between devices with their start and end apart: 5 -> 0, of which waited for: 5 -> 0; matrix products, arithmetic and copies ran while one was open for 2% -> 0% of each run, Pallas kernels for 0% -> 0%
where the time goes in v2:
time: 55.5 us; the launch traced here: 55.4 us
  Pallas kernels  53.7 us (97%)
  local copies, waits for them, and re-layouts  1.67 us (3%)
    pallas_call x1, Pallas kernels, pair_body(): pl.pallas_call(functools.partial(pair_kernel, outer), out_shape=jax.Shape...  53.7 us
    unnamed x1, local copies, waits for them, and re-layouts  1.67 us

profile of v2, /device:TPU:0, one launch (start us, length us, event | category | flops | bytes accessed | tf_op | source)
XLA Modules:
  0.0 55.4 jit_solution(11662793289239981904)
XLA Ops:
  0.0 53.7 %shard_map.55 = f32[32,2048]{1,0:T(8,128)} custom-call(bf16[1,64,2048]{2,1,0:T(8,128)(2,1)} %t_hbm.1, bf16[1,2,64,2048]{3,2,1,0:T(8,128)(2,1)} %r_hbm.1, bf16[32,2048]{1,0:T(8,128)(2,1)} %amp_hbm.1, s32[1,32]{1,0:T(1,128)} %bitcast.4, s32[1,32]{1,0:T(1,128)} %bitcast.5), custom_call_target="tpu_custom_call" | custom-call | tf_op jit(solution)/shard_map/pallas_call | solution.py:428
  53.7 1.7 %copy.7 = f32[1,32,2048]{2,1,0:T(8,128)} copy(f32[1,32,2048]{2,1,0:T(8,128)} %bitcast.3) | data formatting | bytes 524288
